TPU v7x, 32 devices: a whole 2x2x4 slice. The times are simulated.
32 devices in a mesh: clips: 2 (over y), tm: 4 (over z), rows: 2 (over x), cols: 2 (over core).
Axes of the slice: x: 2, y: 2, z: 4, core: 2. Of those that a mesh axis runs over, the one named last changes fastest.
Arguments:
- latent: bfloat16 [16, 4, 64, 384], P(('clips', 'tm'), 'rows', 'cols'), parts along dimension 0, may hold values from -400 to 400, as said below
- norm_gain: float32 [384], replicated, may hold values from 0.1 to 1.9
- time_weight: bfloat16 [3, 384, 768], replicated, may hold values from -0.1875 to 0.1875
- time_bias: float32 [768], replicated, may hold values from -3 to 3
- space_weight: bfloat16 [3, 3, 384, 192], replicated, may hold values from -0.109375 to 0.109375
- space_bias: float32 [192], replicated, may hold values from -3 to 3
Outputs:
- decoded: bfloat16 [32, 8, 128, 192], P(('clips', 'tm'), 'rows', 'cols'), parts along dimension 0
There are 2 independent parts, one for each index of `clips`. A program takes and returns all parts, laid end to end along the dimension named above; an argument that names none is the same for every part. Nothing has to cross between parts.
Inputs may be any that keep to these rules, and one draw needn't show every extreme that they name: `latent`: real-valued activations.
All inputs are finite; a program needn't handle non-finite values.
Results may differ from a plain program's by a relative error of at most 0.0051.
Values may be sent and summed in bfloat16 or wider, within the bound.
A program may use at most 64 MiB of HBM per device.

v0:
```python
import jax
import jax.numpy as jnp
from jax import lax
from jax.sharding import PartitionSpec as P


def passed_along(block, axis, distance):
    devices = range(lax.axis_size(axis))
    route = [(i - distance, i) for i in devices if i - distance in devices]
    return lax.ppermute(block, axis, route)


def with_halo(cells, sides, width):
    for axis, dim in sides:
        count = lax.axis_size(axis)
        ends = count - 1
        head = lax.slice_in_dim(cells, 0, width, axis=dim)
        tail = lax.slice_in_dim(cells, cells.shape[dim] - width, cells.shape[dim], axis=dim)
        cells = jnp.concatenate(
            [
                lax.ppermute(tail, axis, [(i, (i + 1) % count) for i in range(ends)]),
                cells,
                lax.ppermute(head, axis, [((i + 1) % count, i) for i in range(ends)]),
            ],
            axis=dim,
        )
    return cells


def pre_activate(latent, norm_gain):
    values = latent.astype(jnp.float32)
    mean_square = jnp.mean(values * values, axis=-1, keepdims=True)
    scaled = values * lax.rsqrt(mean_square + 1e-06) * norm_gain
    return jax.nn.silu(scaled).astype(jnp.bfloat16)


def time_conv(extended, time_weight, time_bias):
    frames = extended.shape[0] - 2
    height_in = extended.shape[1]
    width_in = extended.shape[2]
    channels = extended.shape[3]
    summed = jnp.zeros((frames * height_in * width_in, time_weight.shape[2]), jnp.float32)
    for offset in range(3):
        window = extended[offset : offset + frames].reshape(-1, channels)
        summed = summed + jnp.dot(window, time_weight[offset], preferred_element_type=jnp.float32)
    summed = summed + time_bias
    return summed.astype(jnp.bfloat16).reshape(frames, height_in, width_in, time_weight.shape[2])


def split_frames(stacked):
    frames, height_in, width_in, doubled = stacked.shape
    channels = doubled // 2
    parted = stacked.reshape(frames, height_in, width_in, 2, channels)
    return jnp.moveaxis(parted, 3, 1).reshape(2 * frames, height_in, width_in, channels)


def space_conv(margined, space_weight, space_bias):
    enlarged = jnp.repeat(jnp.repeat(margined, 2, axis=1), 2, axis=2)[:, 1:-1, 1:-1]
    frames = enlarged.shape[0]
    out_rows = enlarged.shape[1] - 2
    out_cols = enlarged.shape[2] - 2
    channels = enlarged.shape[3]
    summed = jnp.zeros((frames * out_rows * out_cols, space_weight.shape[3]), jnp.float32)
    for row_tap in range(3):
        patches = jnp.concatenate(
            [
                enlarged[:, row_tap : row_tap + out_rows, col_tap : col_tap + out_cols]
                for col_tap in range(3)
            ],
            axis=-1,
        )
        summed = summed + jnp.dot(
            patches.reshape(-1, 3 * channels),
            space_weight[row_tap].reshape(3 * channels, -1),
            preferred_element_type=jnp.float32,
        )
    summed = summed + space_bias
    return summed.astype(jnp.bfloat16).reshape(frames, out_rows, out_cols, space_weight.shape[3])


def local(latent, norm_gain, time_weight, time_bias, space_weight, space_bias):
    activated = pre_activate(latent, norm_gain)
    cached = passed_along(activated, "tm", 1)
    extended = jnp.concatenate([cached, activated], axis=0)
    stacked = time_conv(extended, time_weight, time_bias)
    margined = with_halo(split_frames(stacked), (("rows", 1), ("cols", 2)), 1)
    return space_conv(margined, space_weight, space_bias)


def solution(mesh):
    in_specs = (P(("clips", "tm"), "rows", "cols", None), P(), P(), P(), P(), P())
    out_specs = P(("clips", "tm"), "rows", "cols", None)
    return jax.shard_map(local, mesh=mesh, in_specs=in_specs, out_specs=out_specs, check_vma=False)
```

profile of v0, /device:TPU:9, one launch (start us, length us, event | category | flops | bytes accessed | tf_op | source)
XLA Modules:
  0.0 40.8 jit_solution(18434042265576714465)
XLA Ops:
  0.0 1.0 %fusion.13 = f32[2,2,32]{2,1,0:T(2,128)S(1)} fusion(bf16[2,2,32,384]{3,2,1,0:T(8,128)(2,1)} %param.6), kind=kLoop, calls=%fused_computation.22 | loop fusion | flops 147328 | bytes 98816 | tf_op jit(solution)/shard_map/reduce_sum | solution.py:32
  1.0 1.0 %fusion.20 = bf16[2,2,32,384]{3,2,1,0:T(8,128)(2,1)S(1)} fusion(bf16[2,2,32,384]{3,2,1,0:T(8,128)(2,1)} %param.6, f32[384]{0:T(512)} %param.7, f32[2,2,32]{2,1,0:T(2,128)S(1)} %add_rsqrt_fusion), kind=kLoop, calls=%fused_computation.29 | loop fusion | flops 393216 | bytes 198656 | tf_op jit(solution)/shard_map/convert_element_type | solution.py:34
  2.1 3.2 %collective-permute-start = (bf16[2,2,32,384]{3,2,1,0:T(8,128)(2,1)S(1)}, bf16[2,2,32,384]{3,2,1,0:T(8,128)(2,1)S(1)}, u32[]{:S(2)}, u32[]{:S(2)}) collective-permute-start(bf16[2,2,32,384]{3,2,1,0:T(8,128)(2,1)S(1)} %fusion.20), channel_id=1, source_target_pairs={{0,4},{4,8},{8,12},{1,5},{5,9},{9,13},{2,6},{6,10},{10,14},{3,7},{... | collective-permute-start | bytes 294920 | tf_op jit(solution)/shard_map/ppermute | solution.py:10
  5.3 1.3 %fusion.5 = f32[128,768]{1,0:T(8,128)S(1)} fusion(bf16[128,384]{1,0:T(8,128)(2,1)S(1)} %bitcast.59, bf16[3,384,768]{2,1,0:T(8,128)(2,1)} %param.8), kind=kOutput, calls=%fused_computation.11 | convolution fusion | flops 75497472 | bytes 1081344 | tf_op jit(solution)/shard_map/dot_general | solution.py:45
  6.6 0.8 %collective-permute-done = bf16[2,2,32,384]{3,2,1,0:T(8,128)(2,1)S(1)} collective-permute-done((bf16[2,2,32,384]{3,2,1,0:T(8,128)(2,1)S(1)}, bf16[2,2,32,384]{3,2,1,0:T(8,128)(2,1)S(1)}, u32[]{:S(2)}, u32[]{:S(2)}) %collective-permute-start) | collective-permute-done | bytes 98336 | tf_op jit(solution)/shard_map/ppermute | solution.py:10
  7.4 1.3 %fusion.7 = f32[128,768]{1,0:T(8,128)S(1)} fusion(bf16[128,384]{1,0:T(8,128)(2,1)S(1)} %bitcast.61, bf16[3,384,768]{2,1,0:T(8,128)(2,1)} %param.8), kind=kOutput, calls=%fused_computation.13 | convolution fusion | flops 75497472 | bytes 1081344 | tf_op jit(solution)/shard_map/dot_general | solution.py:45
  8.8 1.3 %fusion.4 = bf16[128,768]{1,0:T(8,128)(2,1)S(1)} fusion(f32[128,768]{1,0:T(8,128)S(1)} %fusion.5, f32[128,768]{1,0:T(8,128)S(1)} %fusion.7, bf16[128,384]{1,0:T(8,128)(2,1)S(1)} %bitcast.60, bf16[3,384,768]{2,1,0:T(8,128)(2,1)} %param.8, f32[768]{0:T(1024)S(1)} %copy-done.1), kind=kOutput, calls=%fused_computation.10 | convolution fusion | flops 75890688 | bytes 1674240 | tf_op jit(solution)/shard_map/dot_general | solution.py:45
  10.2 3.1 %collective-permute-start.1 = (bf16[4,1,32,384]{3,2,1,0:T(8,128)(2,1)S(1)}, bf16[4,1,32,384]{3,2,1,0:T(8,128)(2,1)S(1)}, u32[]{:S(2)}, u32[]{:S(2)}) collective-permute-start(bf16[4,1,32,384]{3,2,1,0:T(8,128)(2,1)S(1)} %get-tuple-element.19), channel_id=1, source_target_pairs={{0,2},{1,3},{4,6},{5,7},{8,10},{9,11},{12,14},{13,15},{16,18},{17,... | collective-permute-start | bytes 294920 | tf_op jit(solution)/shard_map/ppermute | solution.py:21
  13.4 1.3 %collective-permute-start.2 = (bf16[4,1,32,384]{3,2,1,0:T(8,128)(2,1)S(1)}, bf16[4,1,32,384]{3,2,1,0:T(8,128)(2,1)S(1)}, u32[]{:S(2)}, u32[]{:S(2)}) collective-permute-start(bf16[4,1,32,384]{3,2,1,0:T(8,128)(2,1)S(1)} %get-tuple-element.20), channel_id=1, source_target_pairs={{2,0},{3,1},{6,4},{7,5},{10,8},{11,9},{14,12},{15,13},{18,16},{19,... | collective-permute-start | bytes 294920 | tf_op jit(solution)/shard_map/ppermute | solution.py:23
  15.0 3.7 %collective-permute-done.2 = bf16[4,1,32,384]{3,2,1,0:T(8,128)(2,1)S(1)} collective-permute-done((bf16[4,1,32,384]{3,2,1,0:T(8,128)(2,1)S(1)}, bf16[4,1,32,384]{3,2,1,0:T(8,128)(2,1)S(1)}, u32[]{:S(2)}, u32[]{:S(2)}) %collective-permute-start.2) | collective-permute-done | bytes 98336 | tf_op jit(solution)/shard_map/ppermute | solution.py:23
  18.8 1.3 %collective-permute-start.3 = (bf16[4,4,1,384]{3,2,1,0:T(2,128)(2,1)S(1)}, bf16[4,4,1,384]{3,2,1,0:T(2,128)(2,1)S(1)}, u32[]{:S(2)}, u32[]{:S(2)}) collective-permute-start(bf16[4,4,1,384]{3,2,1,0:T(2,128)(2,1)S(1)} %get-tuple-element.17), channel_id=1, source_target_pairs={{0,1},{2,3},{4,5},{6,7},{8,9},{10,11},{12,13},{14,15},{16,17},{18,... | collective-permute-start | bytes 36872 | tf_op jit(solution)/shard_map/ppermute | solution.py:21
  20.1 5.2 %collective-permute-start.4 = (bf16[4,4,1,384]{3,2,1,0:T(2,128)(2,1)S(1)}, bf16[4,4,1,384]{3,2,1,0:T(2,128)(2,1)S(1)}, u32[]{:S(2)}, u32[]{:S(2)}) collective-permute-start(bf16[4,4,1,384]{3,2,1,0:T(2,128)(2,1)S(1)} %get-tuple-element.18), channel_id=1, source_target_pairs={{1,0},{3,2},{5,4},{7,6},{9,8},{11,10},{13,12},{15,14},{17,16},{19,... | collective-permute-start | bytes 36872 | tf_op jit(solution)/shard_map/ppermute | solution.py:23
  25.4 0.4 copy.17
  27.2 0.6 %broadcast_in_dim.4 = bf16[4,4,2,34,384]{4,2,1,3,0:T(2,128)(2,1)S(1)} broadcast(bf16[4,4,34,384]{3,1,2,0:T(4,128)(2,1)S(1)} %copy.15), dimensions={0,1,3,4} | broadcast | bytes 1253376 | tf_op jit(solution)/shard_map/broadcast_in_dim | solution.py:58
  28.2 4.3 %fusion.21 = (bf16[4,4,64,384]{3,1,2,0:T(4,128)(2,1)S(1)}, bf16[4,4,64,384]{3,1,2,0:T(4,128)(2,1)S(1)}, bf16[4,4,64,384]{3,1,2,0:T(4,128)(2,1)S(1)}, bf16[4,4,64...) fusion(bf16[4,8,68,384]{3,1,2,0:T(8,128)(2,1)S(1)} %bitcast.46), kind=kLoop, calls=%fused_computation.35 | loop fusion | bytes 14155776 | tf_op jit(solution)/shard_map/slice | solution.py:67
  32.5 1.1 %pad_maximum_fusion.2 = bf16[4,4,64,1152]{3,1,2,0:T(4,128)(2,1)S(1)} fusion(bf16[4,4,64,384]{3,1,2,0:T(4,128)(2,1)S(1)} %get-tuple-element.6, bf16[4,4,64,384]{3,1,2,0:T(4,128)(2,1)S(1)} %get-tuple-element.7, bf16[4,4,64,384]{3,1,2,0:T(4,128)(2,1)S(1)} %get-tuple-element.5), kind=kLoop, calls=%fused_computation.2 | loop fusion | flops 7077888 | bytes 4718592 | tf_op jit(solution)/shard_map/concatenate | solution.py:65
  33.6 0.4 copy.20
  34.0 2.1 %pad_maximum_fusion = (bf16[4,4,64,1152]{3,1,2,0:T(4,128)(2,1)S(1)}, bf16[4,4,64,1152]{3,1,2,0:T(4,128)(2,1)S(1)}) fusion(bf16[4,4,64,384]{3,1,2,0:T(4,128)(2,1)S(1)} %get-tuple-element.11, bf16[4,4,64,384]{3,1,2,0:T(4,128)(2,1)S(1)} %get-tuple-element.12, bf16[4,4,64,384]{3,1,2,0:T(4,128)(2,1)S(1)} %get-tuple-element.13, ...), kind=kLoop, calls=%fused_computation | loop fusion | flops 14155776 | bytes 9437184 | tf_op jit(solution)/shard_map/concatenate | solution.py:65
  36.2 0.4 copy.16
  36.6 0.4 copy.18
  37.0 0.9 %fusion.24 = f32[1024,192]{0,1:T(8,128)S(1)} fusion(bf16[1024,1152]{1,0:T(8,128)(2,1)S(1)} %bitcast.49, bf16[1152,192]{0,1:T(8,128)(2,1)S(1)} %bitcast.57), kind=kOutput, calls=%fused_computation.38 | convolution fusion | flops 452984832 | bytes 3588096 | tf_op jit(solution)/shard_map/dot_general | solution.py:72
  37.9 0.9 %convolution_add_fusion.1 = f32[1024,192]{0,1:T(8,128)S(1)} fusion(f32[1024,192]{0,1:T(8,128)S(1)} %fusion.24, bf16[1024,1152]{1,0:T(8,128)(2,1)S(1)} %bitcast.47, bf16[1152,192]{0,1:T(8,128)(2,1)S(1)} %bitcast.56), kind=kOutput, calls=%fused_computation.4 | convolution fusion | flops 453181440 | bytes 4374528 | tf_op jit(solution)/shard_map/dot_general | solution.py:72
  38.9 0.9 %fusion.1 = bf16[1024,192]{0,1:T(8,128)(2,1)S(1)} fusion(f32[1024,192]{0,1:T(8,128)S(1)} %convolution_add_fusion.1, bf16[1024,1152]{1,0:T(8,128)(2,1)S(1)} %bitcast.48, bf16[1152,192]{0,1:T(8,128)(2,1)S(1)} %bitcast.58, f32[192]{0:T(256)S(1)} %copy-done.2), kind=kOutput, calls=%fused_computation.6 | convolution fusion | flops 453574656 | bytes 3982080 | tf_op jit(solution)/shard_map/dot_general | solution.py:72
  39.8 1.0 %copy.22 = bf16[1024,192]{1,0:T(8,128)(2,1)} copy(bf16[1024,192]{0,1:T(8,128)(2,1)S(1)} %fusion.1) | data formatting | bytes 786432 | tf_op jit(solution)/shard_map/convert_element_type | solution.py:78
  (25 shorter events, 2.4 us)
Async XLA Ops:
  0.0 8.8 %copy-start.1 = (f32[768]{0:T(1024)S(1)}, f32[768]{0:T(1024)}, u32[]{:S(2)}) copy-start(f32[768]{0:T(1024)} %param.9) | copy-start | bytes 9220
  2.1 5.4 %collective-permute-start = (bf16[2,2,32,384]{3,2,1,0:T(8,128)(2,1)S(1)}, bf16[2,2,32,384]{3,2,1,0:T(8,128)(2,1)S(1)}, u32[]{:S(2)}, u32[]{:S(2)}) collective-permute-start(bf16[2,2,32,384]{3,2,1,0:T(8,128)(2,1)S(1)} %fusion.20), channel_id=1, source_target_pairs={{0,4},{4,8},{8,12},{1,5},{5,9},{9,13},{2,6},{6,10},{10,14},{3,7},{... | collective-permute-start | bytes 294920 | tf_op jit(solution)/shard_map/ppermute | solution.py:10
  6.6 18.6 %copy-start = (bf16[3,3,384,192]{2,3,1,0:T(8,128)(2,1)S(1)}, bf16[3,3,384,192]{2,3,1,0:T(8,128)(2,1)}, u32[]{:S(2)}) copy-start(bf16[3,3,384,192]{2,3,1,0:T(8,128)(2,1)} %param.10) | copy-start | bytes 3981316
  10.2 4.7 %collective-permute-start.1 = (bf16[4,1,32,384]{3,2,1,0:T(8,128)(2,1)S(1)}, bf16[4,1,32,384]{3,2,1,0:T(8,128)(2,1)S(1)}, u32[]{:S(2)}, u32[]{:S(2)}) collective-permute-start(bf16[4,1,32,384]{3,2,1,0:T(8,128)(2,1)S(1)} %get-tuple-element.19), channel_id=1, source_target_pairs={{0,2},{1,3},{4,6},{5,7},{8,10},{9,11},{12,14},{13,15},{16,18},{17,... | collective-permute-start | bytes 294920 | tf_op jit(solution)/shard_map/ppermute | solution.py:21
  13.4 5.4 %collective-permute-start.2 = (bf16[4,1,32,384]{3,2,1,0:T(8,128)(2,1)S(1)}, bf16[4,1,32,384]{3,2,1,0:T(8,128)(2,1)S(1)}, u32[]{:S(2)}, u32[]{:S(2)}) collective-permute-start(bf16[4,1,32,384]{3,2,1,0:T(8,128)(2,1)S(1)} %get-tuple-element.20), channel_id=1, source_target_pairs={{2,0},{3,1},{6,4},{7,5},{10,8},{11,9},{14,12},{15,13},{18,16},{19,... | collective-permute-start | bytes 294920 | tf_op jit(solution)/shard_map/ppermute | solution.py:23
  18.8 8.0 %collective-permute-start.3 = (bf16[4,4,1,384]{3,2,1,0:T(2,128)(2,1)S(1)}, bf16[4,4,1,384]{3,2,1,0:T(2,128)(2,1)S(1)}, u32[]{:S(2)}, u32[]{:S(2)}) collective-permute-start(bf16[4,4,1,384]{3,2,1,0:T(2,128)(2,1)S(1)} %get-tuple-element.17), channel_id=1, source_target_pairs={{0,1},{2,3},{4,5},{6,7},{8,9},{10,11},{12,13},{14,15},{16,17},{18,... | collective-permute-start | bytes 36872 | tf_op jit(solution)/shard_map/ppermute | solution.py:21
  20.1 6.7 %collective-permute-start.4 = (bf16[4,4,1,384]{3,2,1,0:T(2,128)(2,1)S(1)}, bf16[4,4,1,384]{3,2,1,0:T(2,128)(2,1)S(1)}, u32[]{:S(2)}, u32[]{:S(2)}) collective-permute-start(bf16[4,4,1,384]{3,2,1,0:T(2,128)(2,1)S(1)} %get-tuple-element.18), channel_id=1, source_target_pairs={{1,0},{3,2},{5,4},{7,6},{9,8},{11,10},{13,12},{15,14},{17,16},{19,... | collective-permute-start | bytes 36872 | tf_op jit(solution)/shard_map/ppermute | solution.py:23
  37.9 1.0 %copy-start.2 = (f32[192]{0:T(256)S(1)}, f32[192]{0:T(256)}, u32[]{:S(2)}) copy-start(f32[192]{0:T(256)} %param.11) | copy-start | bytes 2308
where the time goes:
time: 41.2 us; the launch traced here: 40.8 us
  starting transfers between devices  14.1 us (34%)
  local copies, waits for them, and re-layouts  9.24 us (22%)
  matrix products  6.81 us (17%)
  other arithmetic  5.52 us (13%)
  waiting for transfers between devices  4.87 us (12%)
    ppermute x2, starting transfers between devices, with_halo(): lax.ppermute(head, axis, [((i + 1) % count, i) for i in range(ends)])  6.45 us
    ppermute x2, starting transfers between devices, with_halo(): lax.ppermute(tail, axis, [(i, (i + 1) % count) for i in range(ends)])  4.41 us
    slice x1, local copies, waits for them, and re-layouts, space_conv(): enlarged[:, row_tap:row_tap + out_rows, col_tap:col_tap + out_cols]  4.29 us
    dot_general x3, matrix products, time_conv(): jnp.dot(window, time_weight[offset], preferred_element_type=jnp.float32)  3.99 us
    ppermute x2, waiting for transfers between devices, with_halo(): lax.ppermute(head, axis, [((i + 1) % count, i) for i in range(ends)])  3.75 us
    ppermute x1, starting transfers between devices, passed_along(): return lax.ppermute(block, axis, route)  3.2 us
    concatenate x2, other arithmetic, space_conv(): jnp.concatenate([enlarged[:, row_tap:row_tap + out_rows, col_tap:col_tap...  3.2 us
    dot_general x3, matrix products, space_conv(): jnp.dot(patches.reshape(-1, 3 * channels), space_weight[row_tap].reshape(...  2.82 us
  transfers between devices with their start and end apart: 5, of which 3 were waited for; matrix products, arithmetic and copies ran while one was open for 7% of the time, Pallas kernels for 0%

commit v1 on v0

v1 whole, which is shorter than its diff:
```python
import functools

import jax
import jax.numpy as jnp
from jax import lax
from jax.experimental import pallas as pl
from jax.experimental.pallas import tpu as pltpu
from jax.sharding import PartitionSpec as P

F32 = jnp.float32
BF16 = jnp.bfloat16
MESH = pl.DeviceIdType.MESH
KINDS = [(dt, dr, dc) for dt in (1, 0) for dr in (0, -1, 1) for dc in (0, 1) if (dt, dr, dc) != (0, 0, 0)]


def activate(raw, gain):
    values = raw.astype(F32)
    mean_square = jnp.mean(values * values, axis=-1, keepdims=True)
    scaled = values * lax.rsqrt(mean_square + 1e-06) * gain
    half = 0.5 * scaled
    return half + half * jnp.tanh(half)


def kernel(tms, nrows, lat_hbm, gain_ref, tw_hbm, tb_ref, sw_hbm, sb_ref, out_ref,
           tile, edge, halo, act, hact, tw, sw, folded, padded, wide, spread, woven,
           load_sem, send_sem, recv_sem):
    frames, height, width, chans = lat_hbm.shape
    couts = sb_ref.shape[1]
    tm = lax.axis_index("tm")
    row = lax.axis_index("rows")
    col = lax.axis_index("cols")
    tall = height + 2

    load_tile = pltpu.make_async_copy(lat_hbm, tile.at[2:, 1 : height + 1], load_sem.at[0])
    load_sw = pltpu.make_async_copy(sw_hbm, sw, load_sem.at[1])
    load_tw = pltpu.make_async_copy(tw_hbm, tw, load_sem.at[2])
    load_tile.start()
    load_sw.start()
    load_tw.start()

    def goes(kind):
        dt, dr, _ = kind
        return (tm + dt < tms) & (row + dr >= 0) & (row + dr < nrows)

    def comes(kind):
        dt, dr, _ = kind
        return (tm - dt >= 0) & (row - dr >= 0) & (row - dr < nrows)

    def count(test):
        return sum(jnp.where(test(kind), 1, 0) for kind in KINDS)

    barrier = pltpu.get_barrier_semaphore()
    for kind in KINDS:
        dt, dr, dc = kind

        @pl.when(comes(kind))
        def _():
            pl.semaphore_signal(
                barrier, inc=1, device_id_type=MESH,
                device_id={"tm": tm - dt, "rows": row - dr, "cols": 1 - col if dc else col})

    def copy_of(index):
        dt, dr, dc = KINDS[index]
        first = frames if dt else 2
        into = 0 if dt else 2
        size = 2 if dt else frames
        source_row, dest_row, rows = {0: (1, 1, height), 1: (height, 0, 1), -1: (1, height + 1, 1)}[dr]
        if dc:
            source = edge.at[pl.ds(first - 2, size), pl.ds(source_row - 1, rows)]
            dest = halo.at[pl.ds(into, size), pl.ds(dest_row, rows)]
        else:
            source = tile.at[pl.ds(first, size), pl.ds(source_row, rows)]
            dest = tile.at[pl.ds(into, size), pl.ds(dest_row, rows)]
        return pltpu.make_async_remote_copy(
            src_ref=source, dst_ref=dest, send_sem=send_sem.at[index], recv_sem=recv_sem.at[index],
            device_id={"tm": tm + dt, "rows": row + dr, "cols": 1 - col if dc else col}, device_id_type=MESH)

    @pl.when(tm == 0)
    def _():
        tile[0:2] = jnp.zeros_like(tile[0:2])
        halo[0:2] = jnp.zeros_like(halo[0:2])

    @pl.when(row == 0)
    def _():
        tile[:, 0:1] = jnp.zeros_like(tile[:, 0:1])
        halo[:, 0:1] = jnp.zeros_like(halo[:, 0:1])

    @pl.when(row == nrows - 1)
    def _():
        tile[:, tall - 1 :] = jnp.zeros_like(tile[:, tall - 1 :])
        halo[:, tall - 1 :] = jnp.zeros_like(halo[:, tall - 1 :])

    load_tile.wait()
    for f in range(frames):
        for i in range(height):
            last = tile[2 + f, 1 + i, width - 16 :, :].astype(F32)[15:16]
            head = tile[2 + f, 1 + i, :16, :].astype(F32)[0:1]
            edge[f, i] = jnp.where(col == 0, last, head)

    pl.semaphore_wait(barrier, count(goes))
    for index, kind in enumerate(KINDS):

        @pl.when(goes(kind))
        def _():
            copy_of(index).start()

    load_sw.wait()
    for b in range(3):
        tap = [sw[a, b].astype(F32) for a in range(3)]
        for p in range(2):
            for r in range(2):
                total = (tap[0], tap[1] + tap[2], tap[0] + tap[1], tap[2])[2 * p + r]
                spread[pl.ds((b * 4 + p * 2 + r) * chans, chans), :] = total
    for p in range(2):
        for r in range(2):
            if folded.shape[-1] > couts:
                folded[p, r, :, :, couts:] = jnp.zeros_like(folded[p, r, :, :, couts:])
            cols_sum = [spread[pl.ds((b * 4 + p * 2 + r) * chans, chans), :] for b in range(3)]
            folded[p, r, 0, :chans, :couts] = cols_sum[0].astype(BF16)
            folded[p, r, 0, chans:, :couts] = (cols_sum[1] + cols_sum[2]).astype(BF16)
            folded[p, r, 1, :chans, :couts] = (cols_sum[0] + cols_sum[1]).astype(BF16)
            folded[p, r, 1, chans:, :couts] = cols_sum[2].astype(BF16)
    load_tw.wait()

    for index, kind in enumerate(KINDS):

        @pl.when(comes(kind))
        def _():
            copy_of(index).wait_recv()

    gain = gain_ref[...]
    for f in range(frames + 2):
        act[f] = activate(tile[f].reshape(tall * width, chans), gain).astype(BF16)
        for i in range(tall):
            hact[pl.ds(f * tall + i, 1), :] = halo[f, i]
    hact[...] = activate(hact[...], gain)

    bias = tb_ref[...]
    count_in = frames * tall
    main = act[...].reshape((frames + 2) * tall * width, chans)
    side = hact[...]
    summed = bias + jnp.zeros((count_in * width, 2 * chans), F32)
    sides = bias + jnp.zeros((count_in, 2 * chans), F32)
    for k in range(3):
        first = k * tall
        weight = tw[k]
        summed += jnp.dot(main[first * width : (first + count_in) * width], weight, preferred_element_type=F32)
        sides += jnp.dot(side[first : first + count_in].astype(BF16), weight, preferred_element_type=F32)
    summed = summed.reshape(count_in, width, 2 * chans)
    for t in range(frames):
        for i in range(tall):
            g = t * tall + i
            center = summed[g]
            rim = sides[g : g + 1]
            if i == 0:
                center = jnp.where(row == 0, 0.0, center)
                rim = jnp.where(row == 0, 0.0, rim)
            if i == tall - 1:
                center = jnp.where(row == nrows - 1, 0.0, center)
                rim = jnp.where(row == nrows - 1, 0.0, rim)
            padded[g, 8 : 8 + width, :] = center
            padded[g, 7:8, :] = jnp.where(col == 0, 0.0, rim)
            padded[g, 8 + width : 9 + width, :] = jnp.where(col == 0, rim, 0.0)
    for t in range(frames):
        for i in range(tall):
            g = t * tall + i
            for shift in range(3):
                moved = padded[g, 7 + shift : 7 + shift + width, :].astype(BF16)
                for s in range(2):
                    wide[2 * t + s, i, :, shift * chans : (shift + 1) * chans] = moved[:, s * chans : (s + 1) * chans]

    cells = 2 * frames * height * width
    for p in range(2):
        for q in range(2):
            total = jnp.zeros((cells, folded.shape[-1]), F32)
            for r in range(2):
                patch = wide[:, p + r : p + r + height, :, q * chans : (q + 2) * chans].reshape(cells, 2 * chans)
                total += jnp.dot(patch, folded[p, r, q], preferred_element_type=F32)
            total = total.reshape(2 * frames, height, width, folded.shape[-1])
            for f in range(2 * frames):
                for i in range(height):
                    base = (f * 2 * height + 2 * i + p) * 2 * width
                    for h in range(woven.shape[0]):
                        woven[h, pl.ds(base + q, width, stride=2), :] = total[f, i, :, h * 128 : (h + 1) * 128]
    for f in range(2 * frames):
        for i in range(2 * height):
            base = (f * 2 * height + i) * 2 * width
            for h in range(woven.shape[0]):
                lanes = slice(h * 128, min(h * 128 + 128, couts))
                size = lanes.stop - lanes.start
                line = woven[h, base : base + 2 * width, :size] + sb_ref[:, lanes]
                out_ref[f, i, :, lanes] = line.astype(BF16)

    for index, kind in enumerate(KINDS):

        @pl.when(goes(kind))
        def _():
            copy_of(index).wait_send()


def local(tms, nrows, latent, norm_gain, time_weight, time_bias, space_weight, space_bias):
    frames, height, width, chans = latent.shape
    couts = space_bias.shape[0]
    tall = height + 2
    groups = frames * tall
    vmem = pl.BlockSpec(memory_space=pltpu.VMEM)
    anywhere = pl.BlockSpec(memory_space=pl.ANY)
    halves = pl.cdiv(couts, 128)
    return pl.pallas_call(
        functools.partial(kernel, tms, nrows),
        name="upsample",
        out_shape=jax.ShapeDtypeStruct((2 * frames, 2 * height, 2 * width, couts), BF16),
        in_specs=[anywhere, vmem, anywhere, vmem, anywhere, vmem],
        out_specs=vmem,
        scratch_shapes=[
            pltpu.VMEM((frames + 2, tall, width, chans), BF16),
            pltpu.VMEM((frames, height, 1, chans), F32),
            pltpu.VMEM((frames + 2, tall, 1, chans), F32),
            pltpu.VMEM((frames + 2, tall * width, chans), BF16),
            pltpu.VMEM(((frames + 2) * tall, chans), F32),
            pltpu.VMEM(time_weight.shape, BF16),
            pltpu.VMEM(space_weight.shape, BF16),
            pltpu.VMEM((2, 2, 2, 2 * chans, halves * 128), BF16),
            pltpu.VMEM((groups, width + 16, 2 * chans), F32),
            pltpu.VMEM((2 * frames, tall, width, 3 * chans), BF16),
            pltpu.VMEM((12 * chans, couts), F32),
            pltpu.VMEM((halves, 8 * frames * height * width, 128), F32),
            pltpu.SemaphoreType.DMA((3,)),
            pltpu.SemaphoreType.DMA((len(KINDS),)),
            pltpu.SemaphoreType.DMA((len(KINDS),)),
        ],
        compiler_params=pltpu.CompilerParams(
            collective_id=0, has_side_effects=True, vmem_limit_bytes=56 * 2**20),
    )(latent, norm_gain[None], time_weight, time_bias[None], space_weight, space_bias[None])


def solution(mesh):
    in_specs = (P(("clips", "tm"), "rows", "cols", None), P(), P(), P(), P(), P())
    out_specs = P(("clips", "tm"), "rows", "cols", None)
    body = functools.partial(local, mesh.shape["tm"], mesh.shape["rows"])
    return jax.shard_map(body, mesh=mesh, in_specs=in_specs, out_specs=out_specs, check_vma=False)
```

time: 41.2 us -> 20 us (0.49)
  starting transfers between devices: 14.1 us -> 0 us
  Pallas kernels: 0 us -> 11.6 us
  matrix products: 6.81 us -> 0 us
  other arithmetic: 5.52 us -> 0 us
  waiting for transfers between devices: 4.87 us -> 0 us
  local copies, waits for them, and re-layouts: 9.24 us -> 8.07 us
    ppermute x5 -> x0, starting transfers between devices: 14.1 us -> none  [the longest x2 6.45 us: with_halo(): lax.ppermute(head, axis, [((i + 1) % count, i) for i in range(ends)])]
    pallas_call x0 -> x1, Pallas kernels: none -> 11.6 us  [local(): pl.pallas_call(functools.partial(kernel, tms, nrows), name='upsample', ou...]
    dot_general x6 -> x0, matrix products: 6.81 us -> none  [the longest x3 3.99 us: time_conv(): jnp.dot(window, time_weight[offset], preferred_element_type=jnp.float32)]
    slice x6 -> x0, local copies, waits for them, and re-layouts: 5.59 us -> none  [the longest x1 4.29 us: space_conv(): enlarged[:, row_tap:row_tap + out_rows, col_tap:col_tap + out_cols]]
    unnamed x9 -> x2, local copies, waits for them, and re-layouts: 0.2 us -> 5.55 us
    ppermute x5 -> x0, waiting for transfers between devices: 4.87 us -> none  [the longest x2 3.75 us: with_halo(): lax.ppermute(head, axis, [((i + 1) % count, i) for i in range(ends)])]
    concatenate x4 -> x0, other arithmetic: 3.45 us -> none  [the longest x2 3.2 us: space_conv(): jnp.concatenate([enlarged[:, row_tap:row_tap + out_rows, col_tap:col_tap...]
    broadcast_in_dim x2, local copies, waits for them, and re-layouts: 0.72 us -> 2.52 us  [the longest x1 1.27 us: local(): time_bias[None]]
  transfers between devices with their start and end apart: 5 -> 0, of which waited for: 3 -> 0; matrix products, arithmetic and copies ran while one was open for 7% -> 0% of each run, Pallas kernels for 0% -> 0%
where the time goes in v1:
time: 20 us; the launch traced here: 19.7 us
  Pallas kernels  11.6 us (58%)
  local copies, waits for them, and re-layouts  8.07 us (40%)
    pallas_call x1, Pallas kernels, local(): pl.pallas_call(functools.partial(kernel, tms, nrows), name='upsample', ou...  11.6 us
    unnamed x2, local copies, waits for them, and re-layouts  5.55 us
    broadcast_in_dim x1, local copies, waits for them, and re-layouts, local(): time_bias[None]  1.27 us
    broadcast_in_dim x1, local copies, waits for them, and re-layouts, local(): norm_gain[None]  1.26 us

profile of v1, /device:TPU:9, one launch (start us, length us, event | category | flops | bytes accessed | tf_op | source)
XLA Modules:
  0.0 19.7 jit_solution(12163380149024444822)
XLA Ops:
  0.0 1.3 %broadcast_in_dim.9.gain_ref = f32[1,384]{1,0:T(1,128)} reshape(f32[384]{0:T(512)} %param.7) | data formatting | bytes 3072 | tf_op jit(solution)/shard_map/broadcast_in_dim | solution.py:234
  1.3 1.3 %broadcast_in_dim.10.tb_ref = f32[1,768]{1,0:T(1,128)} reshape(f32[768]{0:T(1024)} %param.9) | data formatting | bytes 6144 | tf_op jit(solution)/shard_map/broadcast_in_dim | solution.py:234
  2.5 3.7 %copy.7.sw_hbm = bf16[3,3,384,192]{3,2,1,0:T(8,128)(2,1)} copy(bf16[3,3,384,192]{2,3,1,0:T(8,128)(2,1)} %param.10) | data formatting | bytes 2654208 | tf_op args[4]
  6.2 11.6 %upsample.1 = bf16[4,4,64,192]{3,2,1,0:T(8,128)(2,1)} custom-call(bf16[2,2,32,384]{3,2,1,0:T(8,128)(2,1)} %lat_hbm.1, f32[1,384]{1,0:T(1,128)} %broadcast_in_dim.9.gain_ref, bf16[3,384,768]{2,1,0:T(8,128)(2,1)} %tw_hbm.1, f32[1,768]{1,0:T(1,128)} %broadcast_in_dim.10.tb_ref, bf16[3,3,384,192]{3,2,1,0:T(8,128)(2,1)} %copy.7.sw_hbm, f32[1,192]{1,0:T(1,128)} %bitcast.1), custom_call_target="tpu_custom_call" | custom-call | tf_op jit(solution)/shard_map/upsample/pallas_call | solution.py:209
  17.8 1.9 %copy.9 = bf16[4,4,64,192]{3,2,1,0:T(8,128)(2,1)} copy(bf16[4,4,64,192]{3,2,1,0:T(8,128)(2,1)} %upsample.1) | data formatting | bytes 786432

commit v2 on v1

v2 whole, which is shorter than its diff:
```python
import functools

import jax
import jax.numpy as jnp
from jax import lax
from jax.experimental import pallas as pl
from jax.experimental.pallas import tpu as pltpu
from jax.sharding import PartitionSpec as P

F32 = jnp.float32
BF16 = jnp.bfloat16
MESH = pl.DeviceIdType.MESH
KINDS = [
    (frame, dr, dc)
    for frame in (1, None, 0)
    for dc in (0, 1)
    for dr in (0, -1, 1)
    if (frame, dr, dc) != (None, 0, 0)
]


def activate(raw, gain):
    values = raw.astype(F32)
    mean_square = jnp.mean(values * values, axis=-1, keepdims=True)
    scaled = values * lax.rsqrt(mean_square + 1e-06) * gain
    half = 0.5 * scaled
    return half + half * jnp.tanh(half)


def kernel(tms, nrows, lat_hbm, gain_ref, tw_hbm, tb_ref, sw_hbm, sb_ref, out_ref,
           tile, edge, halo, halo_rows, act, acc, tw, sw, folded, padded, wide, woven,
           load_sem, send_sem, recv_sem):
    frames, height, width, chans = lat_hbm.shape
    couts = sb_ref.shape[-1]
    wide_couts = folded.shape[3]
    tm = lax.axis_index("tm")
    row = lax.axis_index("rows")
    col = lax.axis_index("cols")
    tall = height + 2
    cells = tall * width

    load_tile = pltpu.make_async_copy(lat_hbm, tile.at[2:, 1 : height + 1], load_sem.at[0])
    load_sw = pltpu.make_async_copy(sw_hbm, sw, load_sem.at[1])
    load_tw = pltpu.make_async_copy(tw_hbm, tw, load_sem.at[2])
    load_tile.start()
    load_sw.start()
    load_tw.start()

    def goes(kind):
        frame, dr, _ = kind
        return (tm + (frame is not None) < tms) & (row + dr >= 0) & (row + dr < nrows)

    def comes(kind):
        frame, dr, _ = kind
        return (tm - (frame is not None) >= 0) & (row - dr >= 0) & (row - dr < nrows)

    def count(test):
        return sum(jnp.where(test(kind), 1, 0) for kind in KINDS if kind[0] != 0)

    barrier = pltpu.get_barrier_semaphore()
    for kind in KINDS:
        frame, dr, dc = kind
        if frame == 0:
            continue

        @pl.when(comes(kind))
        def _():
            pl.semaphore_signal(
                barrier, inc=1, device_id_type=MESH,
                device_id={"tm": tm - (frame is not None), "rows": row - dr, "cols": 1 - col if dc else col})

    def copy_of(index):
        frame, dr, dc = KINDS[index]
        first, into, size = (2, 2, frames) if frame is None else (frames + frame, frame, 1)
        source_row, dest_row, rows = {0: (1, 1, height), 1: (height, 0, 1), -1: (1, height + 1, 1)}[dr]
        if dc:
            source = edge.at[pl.ds(first - 2, size), pl.ds(source_row - 1, rows)]
            dest = halo.at[pl.ds(into, size), pl.ds(dest_row, rows)]
        else:
            source = tile.at[pl.ds(first, size), pl.ds(source_row, rows)]
            dest = tile.at[pl.ds(into, size), pl.ds(dest_row, rows)]
        return pltpu.make_async_remote_copy(
            src_ref=source, dst_ref=dest, send_sem=send_sem.at[index], recv_sem=recv_sem.at[index],
            device_id={"tm": tm + (frame is not None), "rows": row + dr, "cols": 1 - col if dc else col},
            device_id_type=MESH)

    @pl.when(tm == 0)
    def _():
        tile[0:2] = jnp.zeros_like(tile[0:2])
        halo[0:2] = jnp.zeros_like(halo[0:2])

    @pl.when(row == 0)
    def _():
        tile[:, 0:1] = jnp.zeros_like(tile[:, 0:1])
        halo[:, 0:1] = jnp.zeros_like(halo[:, 0:1])

    @pl.when(row == nrows - 1)
    def _():
        tile[:, tall - 1 :] = jnp.zeros_like(tile[:, tall - 1 :])
        halo[:, tall - 1 :] = jnp.zeros_like(halo[:, tall - 1 :])

    load_tile.wait()
    for f in range(frames):
        for i in range(height):
            last = tile[2 + f, 1 + i, width - 16 :, :].astype(F32)[15:16]
            head = tile[2 + f, 1 + i, :16, :].astype(F32)[0:1]
            edge[f, i] = jnp.where(col == 0, last, head)

    pl.semaphore_wait(barrier, count(goes))
    for index, kind in enumerate(KINDS):

        @pl.when(goes(kind))
        def _():
            copy_of(index).start()

    gain = gain_ref[...].reshape(1, chans)
    halo_rows[...] = jnp.zeros_like(halo_rows)

    def activate_frame(f, begin, end):
        cut = tile[f, begin:end].reshape((end - begin) * width, chans)
        act[begin * width : end * width, f * chans : (f + 1) * chans] = activate(cut, gain).astype(BF16)

    def activate_halo(f):
        for i in range(tall):
            halo_rows[f, i : i + 1, :] = halo[f, i]
        act[cells:, f * chans : (f + 1) * chans] = activate(halo_rows[f], gain).astype(BF16)

    for f in range(frames):
        activate_frame(2 + f, 1, 1 + height)

    if wide_couts > couts:
        for p in range(2):
            for r in range(2):
                for q in range(2):
                    folded[p, r, q, couts:, :] = jnp.zeros((wide_couts - couts, 2 * chans), BF16)
    load_sw.wait()

    def fold(n, carry):
        span = pl.ds(pl.multiple_of(n * 16, 16), 16)
        sums = []
        for b in range(3):
            tap = [sw[a, b, span, :].astype(F32) for a in range(3)]
            sums.append((tap[0], tap[1] + tap[2], tap[0] + tap[1], tap[2]))
        for p in range(2):
            for r in range(2):
                left, middle, right = (sums[b][2 * p + r] for b in range(3))
                folded[p, r, 0, span, :chans] = left.astype(BF16)
                folded[p, r, 0, span, chans:] = (middle + right).astype(BF16)
                folded[p, r, 1, span, :chans] = (left + middle).astype(BF16)
                folded[p, r, 1, span, chans:] = right.astype(BF16)
        return carry

    lax.fori_loop(0, couts // 16, fold, 0)
    load_tw.wait()

    def await_frames(which):
        for index, kind in enumerate(KINDS):
            if kind[0] == which:

                @pl.when(comes(kind))
                def _():
                    copy_of(index).wait_recv()

    def taps(t, begin, end):
        size = (end - begin) * chans
        left = act[:, (t + begin) * chans : (t + end) * chans]
        return jnp.dot(left, tw[begin:end].reshape(size, 2 * chans), preferred_element_type=F32)

    await_frames(None)
    for f in range(frames):
        activate_frame(2 + f, 0, 1)
        activate_frame(2 + f, tall - 1, tall)
        activate_halo(2 + f)
    bias = tb_ref[...].reshape(1, 2 * chans)
    for t in range(frames):
        acc[t] = taps(t, max(2 - t, 0), 3) + bias

    await_frames(1)
    activate_frame(1, 0, tall)
    activate_halo(1)
    stores = []
    for t in reversed(range(frames)):
        if t == 0:
            await_frames(0)
            activate_frame(0, 0, tall)
            activate_halo(0)
        summed = acc[t]
        if t < 2:
            summed += taps(t, 0, 2 - t)
        for i in range(tall):
            center = summed[i * width : (i + 1) * width]
            rim = summed[cells + i : cells + i + 1]
            if i == 0:
                center = jnp.where(row == 0, 0.0, center)
                rim = jnp.where(row == 0, 0.0, rim)
            if i == tall - 1:
                center = jnp.where(row == nrows - 1, 0.0, center)
                rim = jnp.where(row == nrows - 1, 0.0, rim)
            padded[t, i, 8 : 8 + width, :] = center
            padded[t, i, 7:8, :] = jnp.where(col == 0, 0.0, rim)
            padded[t, i, 8 + width : 9 + width, :] = jnp.where(col == 0, rim, 0.0)
            for shift in range(3):
                moved = padded[t, i, 7 + shift : 7 + shift + width, :].astype(BF16)
                for s in range(2):
                    wide[2 * t + s, i, :, shift * chans : (shift + 1) * chans] = moved[:, s * chans : (s + 1) * chans]
        for p in range(2):
            for q in range(2):
                total = jnp.zeros((2 * height * width, wide_couts), F32)
                for r in range(2):
                    patch = wide[2 * t : 2 * t + 2, p + r : p + r + height, :, q * chans : (q + 2) * chans]
                    total += lax.dot_general(
                        patch.reshape(2 * height * width, 2 * chans), folded[p, r, q],
                        (((1,), (1,)), ((), ())), preferred_element_type=F32)
                for s in range(2):
                    for i in range(height):
                        base = ((2 * t + s) * 2 * height + 2 * i + p) * 2 * width
                        part = total[(s * height + i) * width : (s * height + i + 1) * width]
                        for h in range(woven.shape[0]):
                            woven[h, pl.ds(base + q, width, stride=2), :] = part[:, h * 128 : (h + 1) * 128]
        out_bias = sb_ref[...].reshape(1, couts)
        for f in range(2 * t, 2 * t + 2):
            for i in range(2 * height):
                base = (f * 2 * height + i) * 2 * width
                for h in range(woven.shape[0]):
                    lanes = slice(h * 128, min(h * 128 + 128, couts))
                    size = lanes.stop - lanes.start
                    line = woven[h, base : base + 2 * width, :size] + out_bias[:, lanes]
                    out_ref[f, i, :, lanes] = line.astype(BF16)

    for index, kind in enumerate(KINDS):

        @pl.when(goes(kind))
        def _():
            copy_of(index).wait_send()


def local(tms, nrows, latent, norm_gain, time_weight, time_bias, space_weight, space_bias):
    frames, height, width, chans = latent.shape
    couts = space_bias.shape[0]
    tall = height + 2
    spare = 16 * pl.cdiv(tall, 16)
    halves = pl.cdiv(couts, 128)
    vmem = pl.BlockSpec(memory_space=pltpu.VMEM)
    anywhere = pl.BlockSpec(memory_space=pltpu.HBM)
    return pl.pallas_call(
        functools.partial(kernel, tms, nrows),
        name="upsample",
        out_shape=pltpu.VMEM((2 * frames, 2 * height, 2 * width, couts), BF16),
        in_specs=[anywhere, vmem, anywhere, vmem, anywhere, vmem],
        out_specs=vmem,
        scratch_shapes=[
            pltpu.VMEM((frames + 2, tall, width, chans), BF16),
            pltpu.VMEM((frames, height, 1, chans), F32),
            pltpu.VMEM((frames + 2, tall, 1, chans), F32),
            pltpu.VMEM((frames + 2, spare, chans), F32),
            pltpu.VMEM((tall * width + spare, (frames + 2) * chans), BF16),
            pltpu.VMEM((frames, tall * width + spare, 2 * chans), F32),
            pltpu.VMEM(time_weight.shape, BF16),
            pltpu.VMEM((3, 3, couts, chans), BF16),
            pltpu.VMEM((2, 2, 2, halves * 128, 2 * chans), BF16),
            pltpu.VMEM((frames, tall, width + 16, 2 * chans), F32),
            pltpu.VMEM((2 * frames, tall, width, 3 * chans), BF16),
            pltpu.VMEM((halves, 8 * frames * height * width, 128), F32),
            pltpu.SemaphoreType.DMA((3,)),
            pltpu.SemaphoreType.DMA((len(KINDS),)),
            pltpu.SemaphoreType.DMA((len(KINDS),)),
        ],
        compiler_params=pltpu.CompilerParams(
            collective_id=0, has_side_effects=True, vmem_limit_bytes=56 * 2**20),
    )(latent, norm_gain, time_weight, time_bias, jnp.swapaxes(space_weight, 2, 3), space_bias)


def solution(mesh):
    in_specs = (P(("clips", "tm"), "rows", "cols", None), P(), P(), P(), P(), P())
    out_specs = P(("clips", "tm"), "rows", "cols", None)
    body = functools.partial(local, mesh.shape["tm"], mesh.shape["rows"])
    return jax.shard_map(body, mesh=mesh, in_specs=in_specs, out_specs=out_specs, check_vma=False)
```

time: 20 us -> 12.3 us (0.61)
  the two profiles are of different devices: /device:TPU:9 before, /device:TPU:0 now
where the time goes in v2:
time: 12.3 us; the launch traced here: 12.1 us
  Pallas kernels  11.3 us (92%)
  local copies, waits for them, and re-layouts  0.8 us (7%)
    pallas_call x1, Pallas kernels, local(): pl.pallas_call(functools.partial(kernel, tms, nrows), name='upsample', ou...  11.3 us
    unnamed x1, local copies, waits for them, and re-layouts  0.8 us

profile of v2, /device:TPU:0, one launch (start us, length us, event | category | flops | bytes accessed | tf_op | source)
XLA Modules:
  0.0 12.1 jit_solution(15208492396847901794)
XLA Ops:
  0.0 11.3 %upsample.1 = bf16[4,4,64,192]{3,2,1,0:T(8,128)(2,1)S(1)} custom-call(bf16[2,2,32,384]{3,2,1,0:T(8,128)(2,1)} %lat_hbm.1, f32[384]{0:T(512)} %gain_ref.1, bf16[3,384,768]{2,1,0:T(8,128)(2,1)} %tw_hbm.1, f32[768]{0:T(1024)} %tb_ref.1, bf16[3,3,192,384]{3,2,1,0:T(8,128)(2,1)} %bitcast.1, f32[192]{0:T(256)} %sb_ref.1), custom_call_target="tpu_custom_call" | custom-call | tf_op jit(solution)/shard_map/upsample/pallas_call | solution.py:245
  11.3 0.8 %copy.8 = bf16[4,4,64,192]{3,2,1,0:T(8,128)(2,1)} copy(bf16[4,4,64,192]{3,2,1,0:T(8,128)(2,1)S(1)} %upsample.1) | data formatting | bytes 786432

commit v3 on v2

v3 whole, which is shorter than its diff:
```python
import functools

import jax
import jax.numpy as jnp
from jax import lax
from jax.experimental import pallas as pl
from jax.experimental.pallas import tpu as pltpu
from jax.sharding import PartitionSpec as P

F32 = jnp.float32
BF16 = jnp.bfloat16
MESH = pl.DeviceIdType.MESH
KINDS = [(0, dr, 0) for dr in (-1, 1)] + [(1, dr, 0) for dr in (0, -1, 1)]
EDGES = [(dt, dr, 1) for dt in (0, 1) for dr in (0, -1, 1)]
ALL = KINDS + EDGES
GROUPS = [(0, 0), (0, -1), (0, 1), (1, 0), (1, -1), (1, 1)]


def activate(raw, gain):
    values = raw.astype(F32)
    mean_square = jnp.mean(values * values, axis=-1, keepdims=True)
    scaled = values * lax.rsqrt(mean_square + 1e-06) * gain
    half = 0.5 * scaled
    return half + half * jnp.tanh(half)


def kernel(tms, nrows, lat_hbm, gain_ref, tw_hbm, tb_ref, sw_hbm, sb_ref, out_ref,
           tile, edge, halo, halo_rows, act, tw, sw, folded, padded, wide, woven,
           load_sem, send_sem, recv_sem):
    frames, height, width, chans = lat_hbm.shape
    couts = sb_ref.shape[-1]
    wide_couts = folded.shape[3]
    tm = lax.axis_index("tm")
    row = lax.axis_index("rows")
    col = lax.axis_index("cols")
    tall = height + 2
    cells = tall * width

    def when(ok, body):
        if ok is None:
            body()
        else:
            pl.when(ok)(body)

    def goes(dt, dr):
        tests = ([tm < tms - 1] if dt else []) + {0: [], -1: [row > 0], 1: [row < nrows - 1]}[dr]
        return functools.reduce(jnp.logical_and, tests) if tests else None

    def comes(dt, dr):
        tests = ([tm > 0] if dt else []) + {0: [], 1: [row > 0], -1: [row < nrows - 1]}[dr]
        return functools.reduce(jnp.logical_and, tests) if tests else None

    barrier = pltpu.get_barrier_semaphore()
    for dt, dr in GROUPS:

        def signal():
            for dc in (0, 1):
                if (dt, dr, dc) != (0, 0, 0):
                    pl.semaphore_signal(
                        barrier, inc=1, device_id_type=MESH,
                        device_id={"tm": tm - dt, "rows": row - dr, "cols": 1 - col if dc else col})

        when(comes(dt, dr), signal)

    load_tile = pltpu.make_async_copy(lat_hbm, tile.at[2:, 1 : height + 1], load_sem.at[0])
    load_sw = pltpu.make_async_copy(sw_hbm, sw, load_sem.at[1])
    load_tw = pltpu.make_async_copy(tw_hbm, tw, load_sem.at[2])
    load_tile.start()
    load_sw.start()
    load_tw.start()

    def copy_of(kind):
        dt, dr, dc = kind
        first, into, size = (frames - 2, 0, 2) if dt else (0, 2, frames)
        source_row, dest_row, rows = {0: (0, 1, height), 1: (height - 1, 0, 1), -1: (0, height + 1, 1)}[dr]
        source, dest = (edge, halo) if dc else (lat_hbm, tile)
        index = ALL.index(kind)
        return pltpu.make_async_remote_copy(
            src_ref=source.at[pl.ds(first, size), pl.ds(source_row, rows)],
            dst_ref=dest.at[pl.ds(into, size), pl.ds(dest_row, rows)],
            send_sem=send_sem.at[index], recv_sem=recv_sem.at[index],
            device_id={"tm": tm + dt, "rows": row + dr, "cols": 1 - col if dc else col}, device_id_type=MESH)

    vertical = jnp.where(row > 0, 1, 0) + jnp.where(row < nrows - 1, 1, 0)
    pl.semaphore_wait(barrier, 1 + 2 * vertical + jnp.where(tm < tms - 1, 2 + 2 * vertical, 0))
    for kind in KINDS:
        when(goes(*kind[:2]), lambda: copy_of(kind).start())

    load_tile.wait()
    for f in range(frames):
        for i in range(height):
            last = tile[2 + f, 1 + i, width - 16 :, :].astype(F32)[15:16]
            head = tile[2 + f, 1 + i, :16, :].astype(F32)[0:1]
            edge[f, i] = jnp.where(col == 0, last, head)
    for kind in EDGES:
        when(goes(*kind[:2]), lambda: copy_of(kind).start())

    @pl.when(tm == 0)
    def _():
        tile[0:2] = jnp.zeros_like(tile[0:2])
        halo[0:2] = jnp.zeros_like(halo[0:2])

    @pl.when(row == 0)
    def _():
        tile[:, 0:1] = jnp.zeros_like(tile[:, 0:1])
        halo[:, 0:1] = jnp.zeros_like(halo[:, 0:1])

    @pl.when(row == nrows - 1)
    def _():
        tile[:, tall - 1 :] = jnp.zeros_like(tile[:, tall - 1 :])
        halo[:, tall - 1 :] = jnp.zeros_like(halo[:, tall - 1 :])

    gain = gain_ref[...].reshape(1, chans)
    halo_rows[...] = jnp.zeros_like(halo_rows)

    def keep(f, begin, values):
        for k in range(3):
            if 0 <= f - k < frames:
                act[f - k, begin : begin + values.shape[0], k * chans : (k + 1) * chans] = values

    def activate_frame(f, begin, end):
        cut = tile[f, begin:end].reshape((end - begin) * width, chans)
        keep(f, begin * width, activate(cut, gain).astype(BF16))

    def activate_halo(f):
        for i in range(tall):
            halo_rows[f, i : i + 1, :] = halo[f, i]
        keep(f, cells, activate(halo_rows[f], gain).astype(BF16))

    for f in range(frames):
        activate_frame(2 + f, 1, 1 + height)

    if wide_couts > couts:
        for p in range(2):
            for r in range(2):
                for q in range(2):
                    folded[p, r, q, couts:, :] = jnp.zeros((wide_couts - couts, 2 * chans), BF16)
    load_sw.wait()

    def fold(n, carry):
        span = pl.ds(pl.multiple_of(n * 16, 16), 16)
        sums = []
        for b in range(3):
            tap = [sw[a, b, span, :].astype(F32) for a in range(3)]
            sums.append((tap[0], tap[1] + tap[2], tap[0] + tap[1], tap[2]))
        for p in range(2):
            for r in range(2):
                left, middle, right = (sums[b][2 * p + r] for b in range(3))
                folded[p, r, 0, span, :chans] = left.astype(BF16)
                folded[p, r, 0, span, chans:] = (middle + right).astype(BF16)
                folded[p, r, 1, span, :chans] = (left + middle).astype(BF16)
                folded[p, r, 1, span, chans:] = right.astype(BF16)
        return carry

    lax.fori_loop(0, couts // 16, fold, 0)
    load_tw.wait()

    for dt, dr in GROUPS:

        def receive():
            for dc in (0, 1):
                if (dt, dr, dc) != (0, 0, 0):
                    copy_of((dt, dr, dc)).wait_recv()

        when(comes(dt, dr), receive)

    for f in range(frames + 2):
        if f < 2:
            activate_frame(f, 0, tall)
        else:
            activate_frame(f, 0, 1)
            activate_frame(f, tall - 1, tall)
        activate_halo(f)

    span = act.shape[1]
    summed = jnp.dot(
        act[...].reshape(frames * span, 3 * chans), tw[...].reshape(3 * chans, 2 * chans), preferred_element_type=F32)
    summed += tb_ref[...].reshape(1, 2 * chans)
    for t in range(frames):
        for i in range(tall):
            center = summed[t * span + i * width : t * span + (i + 1) * width]
            rim = summed[t * span + cells + i : t * span + cells + i + 1]
            if i == 0:
                center = jnp.where(row == 0, 0.0, center)
                rim = jnp.where(row == 0, 0.0, rim)
            if i == tall - 1:
                center = jnp.where(row == nrows - 1, 0.0, center)
                rim = jnp.where(row == nrows - 1, 0.0, rim)
            padded[t, i, 8 : 8 + width, :] = center
            padded[t, i, 7:8, :] = jnp.where(col == 0, 0.0, rim)
            padded[t, i, 8 + width : 9 + width, :] = jnp.where(col == 0, rim, 0.0)
            for shift in range(3):
                moved = center if shift == 1 else padded[t, i, 7 + shift : 7 + shift + width, :]
                moved = moved.astype(BF16)
                for s in range(2):
                    wide[2 * t + s, i, :, shift * chans : (shift + 1) * chans] = moved[:, s * chans : (s + 1) * chans]

    size = 2 * frames * height * width
    out_bias = sb_ref[...].reshape(1, couts)
    for p in range(2):
        for q in range(2):
            total = jnp.zeros((size, wide_couts), F32)
            for r in range(2):
                patch = wide[:, p + r : p + r + height, :, q * chans : (q + 2) * chans]
                total += lax.dot_general(
                    patch.reshape(size, 2 * chans), folded[p, r, q],
                    (((1,), (1,)), ((), ())), preferred_element_type=F32)
            for f in range(2 * frames):
                for i in range(height):
                    base = (f * 2 * height + 2 * i + p) * 2 * width
                    part = total[(f * height + i) * width : (f * height + i + 1) * width]
                    for h in range(woven.shape[0]):
                        woven[h, pl.ds(base + q, width, stride=2), :] = part[:, h * 128 : (h + 1) * 128]
        for f in range(2 * frames):
            for i in range(p, 2 * height, 2):
                base = (f * 2 * height + i) * 2 * width
                for h in range(woven.shape[0]):
                    lanes = slice(h * 128, min(h * 128 + 128, couts))
                    line = woven[h, base : base + 2 * width, : lanes.stop - lanes.start] + out_bias[:, lanes]
                    out_ref[f, i, :, lanes] = line.astype(BF16)

    for dt, dr in GROUPS:

        def sent():
            for dc in (0, 1):
                if (dt, dr, dc) != (0, 0, 0):
                    copy_of((dt, dr, dc)).wait_send()

        when(goes(dt, dr), sent)


def local(tms, nrows, latent, norm_gain, time_weight, time_bias, space_weight, space_bias):
    frames, height, width, chans = latent.shape
    couts = space_bias.shape[0]
    tall = height + 2
    spare = 16 * pl.cdiv(tall, 16)
    halves = pl.cdiv(couts, 128)
    vmem = pl.BlockSpec(memory_space=pltpu.VMEM)
    anywhere = pl.BlockSpec(memory_space=pltpu.HBM)
    return pl.pallas_call(
        functools.partial(kernel, tms, nrows),
        name="upsample",
        out_shape=pltpu.VMEM((2 * frames, 2 * height, 2 * width, couts), BF16),
        in_specs=[anywhere, vmem, anywhere, vmem, anywhere, vmem],
        out_specs=vmem,
        scratch_shapes=[
            pltpu.VMEM((frames + 2, tall, width, chans), BF16),
            pltpu.VMEM((frames, height, 1, chans), F32),
            pltpu.VMEM((frames + 2, tall, 1, chans), F32),
            pltpu.VMEM((frames + 2, spare, chans), F32),
            pltpu.VMEM((frames, tall * width + spare, 3 * chans), BF16),
            pltpu.VMEM(time_weight.shape, BF16),
            pltpu.VMEM((3, 3, couts, chans), BF16),
            pltpu.VMEM((2, 2, 2, halves * 128, 2 * chans), BF16),
            pltpu.VMEM((frames, tall, width + 16, 2 * chans), F32),
            pltpu.VMEM((2 * frames, tall, width, 3 * chans), BF16),
            pltpu.VMEM((halves, 8 * frames * height * width, 128), F32),
            pltpu.SemaphoreType.DMA((3,)),
            pltpu.SemaphoreType.DMA((len(ALL),)),
            pltpu.SemaphoreType.DMA((len(ALL),)),
        ],
        compiler_params=pltpu.CompilerParams(
            collective_id=0, has_side_effects=True, vmem_limit_bytes=56 * 2**20),
    )(latent, norm_gain, time_weight, time_bias, jnp.swapaxes(space_weight, 2, 3), space_bias)


def solution(mesh):
    in_specs = (P(("clips", "tm"), "rows", "cols", None), P(), P(), P(), P(), P())
    out_specs = P(("clips", "tm"), "rows", "cols", None)
    body = functools.partial(local, mesh.shape["tm"], mesh.shape["rows"])
    return jax.shard_map(body, mesh=mesh, in_specs=in_specs, out_specs=out_specs, check_vma=False)
```

time: 12.3 us -> 11.7 us (0.951)
  the two profiles are of different devices: /device:TPU:0 before, /device:TPU:9 now
where the time goes in v3:
time: 11.7 us; the launch traced here: 11.6 us
  Pallas kernels  10.8 us (92%)
  local copies, waits for them, and re-layouts  0.8 us (7%)
    pallas_call x1, Pallas kernels, local(): pl.pallas_call(functools.partial(kernel, tms, nrows), name='upsample', ou...  10.8 us
    unnamed x1, local copies, waits for them, and re-layouts  0.8 us

profile of v3, /device:TPU:9, one launch (start us, length us, event | category | flops | bytes accessed | tf_op | source)
XLA Modules:
  0.0 11.6 jit_solution(5115371324230395442)
XLA Ops:
  0.0 10.8 %upsample.1 = bf16[4,4,64,192]{3,2,1,0:T(8,128)(2,1)S(1)} custom-call(bf16[2,2,32,384]{3,2,1,0:T(8,128)(2,1)} %lat_hbm.1, f32[384]{0:T(512)} %gain_ref.1, bf16[3,384,768]{2,1,0:T(8,128)(2,1)} %tw_hbm.1, f32[768]{0:T(1024)} %tb_ref.1, bf16[3,3,192,384]{3,2,1,0:T(8,128)(2,1)} %bitcast.1, f32[192]{0:T(256)} %sb_ref.1), custom_call_target="tpu_custom_call" | custom-call | tf_op jit(solution)/shard_map/upsample/pallas_call | solution.py:240
  10.8 0.8 %copy.8 = bf16[4,4,64,192]{3,2,1,0:T(8,128)(2,1)} copy(bf16[4,4,64,192]{3,2,1,0:T(8,128)(2,1)S(1)} %upsample.1) | data formatting | bytes 786432

commit v4 on v3

--- a/solution.py
+++ b/solution.py
@@ -10,7 +10,7 @@
 F32 = jnp.float32
 BF16 = jnp.bfloat16
 MESH = pl.DeviceIdType.MESH
-KINDS = [(0, dr, 0) for dr in (-1, 1)] + [(1, dr, 0) for dr in (0, -1, 1)]
+KINDS = [(1, 0, 0), (0, -1, 0), (0, 1, 0), (1, -1, 0), (1, 1, 0)]
 EDGES = [(dt, dr, 1) for dt in (0, 1) for dr in (0, -1, 1)]
 ALL = KINDS + EDGES
 GROUPS = [(0, 0), (0, -1), (0, 1), (1, 0), (1, -1), (1, 1)]
@@ -25,7 +25,7 @@
 
 
 def kernel(tms, nrows, lat_hbm, gain_ref, tw_hbm, tb_ref, sw_hbm, sb_ref, out_ref,
-           tile, edge, halo, halo_rows, act, tw, sw, folded, padded, wide, woven,
+           tile, edge, halo, halo_rows, act, acc, tw, sw, folded, padded, wide, woven,
            load_sem, send_sem, recv_sem):
     frames, height, width, chans = lat_hbm.shape
     couts = sb_ref.shape[-1]
@@ -155,27 +155,37 @@
     lax.fori_loop(0, couts // 16, fold, 0)
     load_tw.wait()
 
-    for dt, dr in GROUPS:
-
-        def receive():
-            for dc in (0, 1):
-                if (dt, dr, dc) != (0, 0, 0):
-                    copy_of((dt, dr, dc)).wait_recv()
-
-        when(comes(dt, dr), receive)
-
-    for f in range(frames + 2):
-        if f < 2:
-            activate_frame(f, 0, tall)
-        else:
-            activate_frame(f, 0, 1)
-            activate_frame(f, tall - 1, tall)
+    def await_groups(step):
+        for dt, dr in GROUPS:
+
+            def receive():
+                for dc in (0, 1):
+                    if (dt, dr, dc) != (0, 0, 0):
+                        copy_of((dt, dr, dc)).wait_recv()
+
+            if dt == step:
+                when(comes(dt, dr), receive)
+
+    span = act.shape[1]
+
+    def taps(begin, end):
+        size = (end - begin) * chans
+        return jnp.dot(
+            act[:, :, begin * chans : end * chans].reshape(frames * span, size),
+            tw[begin:end].reshape(size, 2 * chans), preferred_element_type=F32)
+
+    await_groups(0)
+    for f in range(2, frames + 2):
+        activate_frame(f, 0, 1)
+        activate_frame(f, tall - 1, tall)
         activate_halo(f)
-
-    span = act.shape[1]
-    summed = jnp.dot(
-        act[...].reshape(frames * span, 3 * chans), tw[...].reshape(3 * chans, 2 * chans), preferred_element_type=F32)
-    summed += tb_ref[...].reshape(1, 2 * chans)
+    acc[...] = taps(2, 3) + tb_ref[...].reshape(1, 2 * chans)
+
+    await_groups(1)
+    for f in range(2):
+        activate_frame(f, 0, tall)
+        activate_halo(f)
+    summed = acc[...] + taps(0, 2)
     for t in range(frames):
         for i in range(tall):
             center = summed[t * span + i * width : t * span + (i + 1) * width]
@@ -249,6 +259,7 @@
             pltpu.VMEM((frames + 2, tall, 1, chans), F32),
             pltpu.VMEM((frames + 2, spare, chans), F32),
             pltpu.VMEM((frames, tall * width + spare, 3 * chans), BF16),
+            pltpu.VMEM((frames * (tall * width + spare), 2 * chans), F32),
             pltpu.VMEM(time_weight.shape, BF16),
             pltpu.VMEM((3, 3, couts, chans), BF16),
             pltpu.VMEM((2, 2, 2, halves * 128, 2 * chans), BF16),

time: 11.7 us -> 11.5 us (0.983)
  Pallas kernels: 10.8 us -> 10.5 us
    pallas_call x1, Pallas kernels: 10.8 us -> 10.5 us  [local(): pl.pallas_call(functools.partial(kernel, tms, nrows), name='upsample', ou...]
where the time goes in v4:
time: 11.5 us; the launch traced here: 11.3 us
  Pallas kernels  10.5 us (91%)
  local copies, waits for them, and re-layouts  0.8 us (7%)
    pallas_call x1, Pallas kernels, local(): pl.pallas_call(functools.partial(kernel, tms, nrows), name='upsample', ou...  10.5 us
    unnamed x1, local copies, waits for them, and re-layouts  0.8 us

profile of v4, /device:TPU:9, one launch (start us, length us, event | category | flops | bytes accessed | tf_op | source)
XLA Modules:
  0.0 11.3 jit_solution(3607452344724549486)
XLA Ops:
  0.0 10.5 %upsample.1 = bf16[4,4,64,192]{3,2,1,0:T(8,128)(2,1)S(1)} custom-call(bf16[2,2,32,384]{3,2,1,0:T(8,128)(2,1)} %lat_hbm.1, f32[384]{0:T(512)} %gain_ref.1, bf16[3,384,768]{2,1,0:T(8,128)(2,1)} %tw_hbm.1, f32[768]{0:T(1024)} %tb_ref.1, bf16[3,3,192,384]{3,2,1,0:T(8,128)(2,1)} %bitcast.1, f32[192]{0:T(256)} %sb_ref.1), custom_call_target="tpu_custom_call" | custom-call | tf_op jit(solution)/shard_map/upsample/pallas_call | solution.py:250
  10.5 0.8 %copy.8 = bf16[4,4,64,192]{3,2,1,0:T(8,128)(2,1)} copy(bf16[4,4,64,192]{3,2,1,0:T(8,128)(2,1)S(1)} %upsample.1) | data formatting | bytes 786432

commit v5 on v4

--- a/solution.py
+++ b/solution.py
@@ -118,9 +118,14 @@
             if 0 <= f - k < frames:
                 act[f - k, begin : begin + values.shape[0], k * chans : (k + 1) * chans] = values
 
+    own = height * width
+
+    def place(i):
+        return own if i == 0 else own + width if i == tall - 1 else (i - 1) * width
+
     def activate_frame(f, begin, end):
         cut = tile[f, begin:end].reshape((end - begin) * width, chans)
-        keep(f, begin * width, activate(cut, gain).astype(BF16))
+        keep(f, place(begin), activate(cut, gain).astype(BF16))
 
     def activate_halo(f):
         for i in range(tall):
@@ -155,55 +160,70 @@
     lax.fori_loop(0, couts // 16, fold, 0)
     load_tw.wait()
 
-    def await_groups(step):
-        for dt, dr in GROUPS:
+    def await_groups(groups):
+        for dt, dr in groups:
 
             def receive():
                 for dc in (0, 1):
                     if (dt, dr, dc) != (0, 0, 0):
                         copy_of((dt, dr, dc)).wait_recv()
 
-            if dt == step:
-                when(comes(dt, dr), receive)
+            when(comes(dt, dr), receive)
+
+    def taps(begin, end, low, high):
+        depth = (end - begin) * chans
+        product = jnp.dot(
+            act[:, low:high, begin * chans : end * chans].reshape(frames * (high - low), depth),
+            tw[begin:end].reshape(depth, 2 * chans), preferred_element_type=F32)
+        return product.reshape(frames, high - low, 2 * chans)
+
+    def put(t, i, shift, values):
+        values = values.astype(BF16)
+        for s in range(2):
+            wide[2 * t + s, i, :, shift * chans : (shift + 1) * chans] = values[:, s * chans : (s + 1) * chans]
+
+    def inside(i, values):
+        if i == 0:
+            return jnp.where(row == 0, 0.0, values)
+        if i == tall - 1:
+            return jnp.where(row == nrows - 1, 0.0, values)
+        return values
 
     span = act.shape[1]
-
-    def taps(begin, end):
-        size = (end - begin) * chans
-        return jnp.dot(
-            act[:, :, begin * chans : end * chans].reshape(frames * span, size),
-            tw[begin:end].reshape(size, 2 * chans), preferred_element_type=F32)
-
-    await_groups(0)
+    await_groups([(0, 0), (0, -1), (0, 1)])
     for f in range(2, frames + 2):
         activate_frame(f, 0, 1)
         activate_frame(f, tall - 1, tall)
         activate_halo(f)
-    acc[...] = taps(2, 3) + tb_ref[...].reshape(1, 2 * chans)
-
-    await_groups(1)
+    acc[...] = taps(2, 3, 0, span) + tb_ref[...].reshape(1, 1, 2 * chans)
+
+    await_groups([(1, 0)])
     for f in range(2):
-        activate_frame(f, 0, tall)
+        activate_frame(f, 1, 1 + height)
+    summed = acc[:, :own] + taps(0, 2, 0, own)
+    for t in range(frames):
+        for i in range(1, 1 + height):
+            center = summed[t, place(i) : place(i) + width]
+            padded[t, i, 8 : 8 + width, :] = center
+            put(t, i, 1, center)
+
+    await_groups([(1, -1), (1, 1)])
+    for f in range(2):
+        activate_frame(f, 0, 1)
+        activate_frame(f, tall - 1, tall)
         activate_halo(f)
-    summed = acc[...] + taps(0, 2)
+    summed = acc[:, own:] + taps(0, 2, own, span)
     for t in range(frames):
         for i in range(tall):
-            center = summed[t * span + i * width : t * span + (i + 1) * width]
-            rim = summed[t * span + cells + i : t * span + cells + i + 1]
-            if i == 0:
-                center = jnp.where(row == 0, 0.0, center)
-                rim = jnp.where(row == 0, 0.0, rim)
-            if i == tall - 1:
-                center = jnp.where(row == nrows - 1, 0.0, center)
-                rim = jnp.where(row == nrows - 1, 0.0, rim)
-            padded[t, i, 8 : 8 + width, :] = center
+            if i in (0, tall - 1):
+                center = inside(i, summed[t, place(i) - own : place(i) - own + width])
+                padded[t, i, 8 : 8 + width, :] = center
+                put(t, i, 1, center)
+            rim = inside(i, summed[t, 2 * width + i : 2 * width + i + 1])
             padded[t, i, 7:8, :] = jnp.where(col == 0, 0.0, rim)
             padded[t, i, 8 + width : 9 + width, :] = jnp.where(col == 0, rim, 0.0)
-            for shift in range(3):
-                moved = center if shift == 1 else padded[t, i, 7 + shift : 7 + shift + width, :]
-                moved = moved.astype(BF16)
-                for s in range(2):
-                    wide[2 * t + s, i, :, shift * chans : (shift + 1) * chans] = moved[:, s * chans : (s + 1) * chans]
+            for shift in (0, 2):
+                put(t, i, shift, padded[t, i, 7 + shift : 7 + shift + width, :])
 
     size = 2 * frames * height * width
     out_bias = sb_ref[...].reshape(1, couts)
@@ -259,7 +279,7 @@
             pltpu.VMEM((frames + 2, tall, 1, chans), F32),
             pltpu.VMEM((frames + 2, spare, chans), F32),
             pltpu.VMEM((frames, tall * width + spare, 3 * chans), BF16),
-            pltpu.VMEM((frames * (tall * width + spare), 2 * chans), F32),
+            pltpu.VMEM((frames, tall * width + spare, 2 * chans), F32),
             pltpu.VMEM(time_weight.shape, BF16),
             pltpu.VMEM((3, 3, couts, chans), BF16),
             pltpu.VMEM((2, 2, 2, halves * 128, 2 * chans), BF16),

time: 11.5 us -> 11.8 us (1.026)
  Pallas kernels: 10.5 us -> 10.8 us
    pallas_call x1, Pallas kernels: 10.5 us -> 10.8 us  [local(): pl.pallas_call(functools.partial(kernel, tms, nrows), name='upsample', ou...]
where the time goes in v5:
time: 11.8 us; the launch traced here: 11.6 us
  Pallas kernels  10.8 us (92%)
  local copies, waits for them, and re-layouts  0.8 us (7%)
    pallas_call x1, Pallas kernels, local(): pl.pallas_call(functools.partial(kernel, tms, nrows), name='upsample', ou...  10.8 us
    unnamed x1, local copies, waits for them, and re-layouts  0.8 us

profile of v5, /device:TPU:9, one launch (start us, length us, event | category | flops | bytes accessed | tf_op | source)
XLA Modules:
  0.0 11.6 jit_solution(12247363753217519394)
XLA Ops:
  0.0 10.8 %upsample.1 = bf16[4,4,64,192]{3,2,1,0:T(8,128)(2,1)S(1)} custom-call(bf16[2,2,32,384]{3,2,1,0:T(8,128)(2,1)} %lat_hbm.1, f32[384]{0:T(512)} %gain_ref.1, bf16[3,384,768]{2,1,0:T(8,128)(2,1)} %tw_hbm.1, f32[768]{0:T(1024)} %tb_ref.1, bf16[3,3,192,384]{3,2,1,0:T(8,128)(2,1)} %bitcast.1, f32[192]{0:T(256)} %sb_ref.1), custom_call_target="tpu_custom_call" | custom-call | tf_op jit(solution)/shard_map/upsample/pallas_call | solution.py:270
  10.8 0.8 %copy.8 = bf16[4,4,64,192]{3,2,1,0:T(8,128)(2,1)} copy(bf16[4,4,64,192]{3,2,1,0:T(8,128)(2,1)S(1)} %upsample.1) | data formatting | bytes 786432

commit v6 on v5

--- a/solution.py
+++ b/solution.py
@@ -83,7 +83,7 @@
 
     vertical = jnp.where(row > 0, 1, 0) + jnp.where(row < nrows - 1, 1, 0)
     pl.semaphore_wait(barrier, 1 + 2 * vertical + jnp.where(tm < tms - 1, 2 + 2 * vertical, 0))
-    for kind in KINDS:
+    for kind in KINDS[:3]:
         when(goes(*kind[:2]), lambda: copy_of(kind).start())
 
     load_tile.wait()
@@ -92,7 +92,7 @@
             last = tile[2 + f, 1 + i, width - 16 :, :].astype(F32)[15:16]
             head = tile[2 + f, 1 + i, :16, :].astype(F32)[0:1]
             edge[f, i] = jnp.where(col == 0, last, head)
-    for kind in EDGES:
+    for kind in EDGES + KINDS[3:]:
         when(goes(*kind[:2]), lambda: copy_of(kind).start())
 
     @pl.when(tm == 0)

time: 11.8 us -> 11.5 us (0.975)
  the two profiles are of different devices: /device:TPU:9 before, /device:TPU:0 now
where the time goes in v6:
time: 11.5 us; the launch traced here: 11.3 us
  Pallas kernels  10.5 us (91%)
  local copies, waits for them, and re-layouts  0.8 us (7%)
    pallas_call x1, Pallas kernels, local(): pl.pallas_call(functools.partial(kernel, tms, nrows), name='upsample', ou...  10.5 us
    unnamed x1, local copies, waits for them, and re-layouts  0.8 us

profile of v6, /device:TPU:0, one launch (start us, length us, event | category | flops | bytes accessed | tf_op | source)
XLA Modules:
  0.0 11.3 jit_solution(13883507356537746489)
XLA Ops:
  0.0 10.5 %upsample.1 = bf16[4,4,64,192]{3,2,1,0:T(8,128)(2,1)S(1)} custom-call(bf16[2,2,32,384]{3,2,1,0:T(8,128)(2,1)} %lat_hbm.1, f32[384]{0:T(512)} %gain_ref.1, bf16[3,384,768]{2,1,0:T(8,128)(2,1)} %tw_hbm.1, f32[768]{0:T(1024)} %tb_ref.1, bf16[3,3,192,384]{3,2,1,0:T(8,128)(2,1)} %bitcast.1, f32[192]{0:T(256)} %sb_ref.1), custom_call_target="tpu_custom_call" | custom-call | tf_op jit(solution)/shard_map/upsample/pallas_call | solution.py:270
  10.5 0.8 %copy.8 = bf16[4,4,64,192]{3,2,1,0:T(8,128)(2,1)} copy(bf16[4,4,64,192]{3,2,1,0:T(8,128)(2,1)S(1)} %upsample.1) | data formatting | bytes 786432
